TPU v7x, 32 devices: a whole 2x2x4 slice. The times are simulated.
32 devices in a mesh: inp: 2 (over x), tm: 16 (over z, y, core).
Axes of the slice: x: 2, y: 2, z: 4, core: 2. Of those that a mesh axis runs over, the one named last changes fastest.
Arguments:
- samples: int32 [512, 524288], P('inp', 'tm'), may hold values from -8 to 7
- filter_taps: int32 [4, 2048], replicated, may hold values from -4096 to 4095
Outputs:
- visibilities: float32 [2, 1024, 512, 512], P(None, ('inp', 'tm'))
All inputs are finite; a program needn't handle non-finite values.
Results may differ from a plain program's by a relative error of at most 0.0032.
Values may be sent and summed in bfloat16 or wider, within the bound.
No kernel may reach another device: no remote copies, remote signals or barrier semaphores. Data moves between devices by JAX's collectives and lax.ppermute only.
A program may use at most 256 MiB of HBM per device.

v0:
```python
import math

import jax
import jax.numpy as jnp
from jax import lax
from jax.sharding import PartitionSpec as P

BLOCKS = 4
SPEC_BLK = 4


def shifted(value, axis, steps):
    count = lax.axis_size(axis)
    initial, last = (max(0, -steps), min(count, count - steps))
    return lax.ppermute(value, axis, [(source, source + steps) for source in range(initial, last)])


def dft_table(frame_len, channels):
    points = lax.broadcasted_iota(jnp.int32, (channels, frame_len), 1)
    freqs = lax.broadcasted_iota(jnp.int32, (channels, frame_len), 0)
    angle = (points * freqs % frame_len).astype(jnp.float32) * (2.0 * math.pi / frame_len)
    scale = 1.0 / math.sqrt(frame_len)
    paired = jnp.stack([jnp.cos(angle) * scale, -jnp.sin(angle) * scale], axis=1)
    return paired.reshape(2 * channels, frame_len)


def on_device(samples, filter_taps):
    local_inputs = samples.shape[0]
    tap_count = filter_taps.shape[0]
    frame_len = filter_taps.shape[1]
    spec_dev = samples.shape[1] // frame_len
    channels = frame_len // 2
    inp_count = lax.axis_size("inp")
    tm_count = lax.axis_size("tm")
    all_inputs = local_inputs * inp_count
    chan_dev = channels // (inp_count * tm_count)
    total_spectra = spec_dev * tm_count
    row_width = 2 * SPEC_BLK * local_inputs
    frames = jnp.transpose(samples.reshape(local_inputs, spec_dev, frame_len), (1, 0, 2)).astype(
        jnp.bfloat16
    )
    history = shifted(frames[spec_dev - (tap_count - 1) :], "tm", 1)
    extended = jnp.concatenate([history, frames], axis=0)
    weights = filter_taps.astype(jnp.float32) / 16384.0
    table = dft_table(frame_len, channels)
    highest = lax.Precision.HIGHEST
    collected = []
    for block in range(BLOCKS):
        first = block * SPEC_BLK
        window = extended[first : first + SPEC_BLK + tap_count - 1].astype(jnp.float32)
        filtered = jnp.zeros((SPEC_BLK, local_inputs, frame_len), jnp.float32)
        for offset in range(tap_count):
            filtered = filtered + weights[offset] * window[offset : offset + SPEC_BLK]
        filtered = lax.optimization_barrier(filtered.astype(jnp.bfloat16)).astype(jnp.float32)
        filtered = filtered.reshape(SPEC_BLK * local_inputs, frame_len)
        spectra = lax.dot_general(table, filtered, (((1,), (1,)), ((), ())), precision=highest)
        spectra = spectra.reshape(channels, row_width)
        pieces = spectra.reshape(inp_count * tm_count, chan_dev, row_width)
        arrived = lax.all_to_all(pieces, ("inp", "tm"), split_axis=0, concat_axis=0, tiled=True)
        collected.append(arrived.reshape(inp_count, tm_count, chan_dev, 2, SPEC_BLK, local_inputs))
    gathered = jnp.stack(collected, axis=0)
    ordered = jnp.transpose(gathered, (3, 4, 0, 2, 5, 1, 6))
    ordered = ordered.reshape(chan_dev, 2, BLOCKS * tm_count * SPEC_BLK, all_inputs)
    power = jnp.einsum("cpma,cpmb->cab", ordered, ordered, precision=highest)
    cross = jnp.einsum("cma,cmb->cab", ordered[:, 1], ordered[:, 0], precision=highest)
    phase = cross - jnp.transpose(cross, (0, 2, 1))
    return jnp.stack([power, phase]) / total_spectra


def solution(mesh):
    placed = (P("inp", "tm"), P())
    return jax.shard_map(
        on_device,
        mesh=mesh,
        in_specs=placed,
        out_specs=P(None, ("inp", "tm"), None, None),
        check_vma=False,
    )
```

profile of v0, /device:TPU:0, one launch (start us, length us, event | category | flops | bytes accessed | tf_op | source)
XLA Modules:
  0.0 1302.4 jit_solution(16092905250027546708)
XLA Ops:
  0.0 33.4 %copy.42 = s32[256,32768]{0,1:T(8,128)} copy(s32[256,32768]{1,0:T(8,128)} %param.2) | data formatting | bytes 67108864 | tf_op args[0]
  33.4 12.2 convert_element_type.58
  50.2 34.9 %negate_multiply_fusion = (f32[1024,1,2048]{2,0,1:T(8,128)}, f32[1024,1,2048]{2,0,1:T(8,128)}) fusion(), kind=kLoop, calls=%fused_computation.47 | loop fusion | flops 35651584 | bytes 16777216 | tf_op jit(solution)/shard_map/mul | solution.py:23
  91.6 21.3 %copy.41 = f32[1024,2,2048]{2,1,0:T(2,128)} copy(f32[1024,2,2048]{2,0,1:T(8,128)S(1)} %pad_maximum_fusion) | data formatting | bytes 33554432 | tf_op jit(solution)/shard_map/stack | solution.py:23
  113.0 20.5 %reshape.91 = f32[2048,2048]{1,0:T(8,128)} reshape(f32[1024,2,2048]{2,1,0:T(2,128)} %copy.41) | data formatting | bytes 33554432 | tf_op jit(solution)/shard_map/reshape | solution.py:24
  133.6 27.4 %fusion.24 = (f32[7,256,2048]{1,2,0:T(8,128)}, f32[7,256,2048]{1,2,0:T(8,128)}, f32[7,256,2048]{1,2,0:T(8,128)}, f32[7,256,2048]{1,2,0:T(8,128)}) fusion(bf16[16,256,2048]{1,2,0:T(8,128)(2,1)} %bitcast.40, bf16[3,256,2048]{1,2,0:T(8,128)(2,1)S(1)} %collective-permute-done), kind=kLoop, calls=%fused_computation.56 | loop fusion | flops 18350080 | bytes 100663296 | tf_op jit(solution)/shard_map/convert_element_type | solution.py:50
  160.9 38.7 %fusion.18 = (bf16[4,256,2048]{1,2,0:T(8,128)(2,1)}, bf16[4,256,2048]{1,2,0:T(8,128)(2,1)}, bf16[4,256,2048]{1,2,0:T(8,128)(2,1)}) fusion(f32[7,256,2048]{1,2,0:T(8,128)} %get-tuple-element.5, f32[2048]{0:T(1024)S(1)} %bitcast.47, f32[2048]{0:T(1024)S(1)} %bitcast.49, f32[2048]{0:T(1024)S(1)} %bitcast.51, f32[2048]{0:T(1024)S(1)} %bitcast.45, ...), kind=kLoop, calls=%fused_computation.41 | loop fusion | flops 50331648 | bytes 113278976 | tf_op jit(solution)/shard_map/convert_element_type | solution.py:54
  205.9 31.7 %fusion.27 = f32[2048,1024]{1,0:T(8,128)} fusion(f32[2048,2048]{1,0:T(8,128)} %reshape.91, bf16[1024,2048]{1,0:T(8,128)(2,1)} %bitcast.42), kind=kOutput, calls=%fused_computation.60 | convolution fusion | flops 51539607552 | bytes 29360128 | tf_op jit(solution)/shard_map/dot_general | solution.py:56
  237.6 10.0 reshape_reshape.13
  261.2 31.6 %fusion.26 = f32[2048,1024]{1,0:T(8,128)} fusion(f32[2048,2048]{1,0:T(8,128)} %reshape.91, bf16[1024,2048]{1,0:T(8,128)(2,1)} %bitcast.43), kind=kOutput, calls=%fused_computation.59 | convolution fusion | flops 51539607552 | bytes 29360128 | tf_op jit(solution)/shard_map/dot_general | solution.py:56
  302.6 137.0 %all-to-all-done.1 = f32[32,32,2048]{2,1,0:T(8,128)} async-done(((f32[32,32,2048]{2,1,0:T(8,128)}), f32[32,32,2048]{2,1,0:T(8,128)}, u32[]{:S(2)}, u32[]{:S(2)}) %all-to-all-start.1) | async-done | bytes 8388640 | tf_op jit(solution)/shard_map/all_to_all | solution.py:59
  449.9 31.6 %fusion.28 = f32[2048,1024]{1,0:T(8,128)} fusion(f32[2048,2048]{1,0:T(8,128)} %reshape.91, bf16[1024,2048]{1,0:T(8,128)(2,1)} %bitcast.44), kind=kOutput, calls=%fused_computation.61 | convolution fusion | flops 51539607552 | bytes 29360128 | tf_op jit(solution)/shard_map/dot_general | solution.py:56
  491.4 136.9 %all-to-all-done = f32[32,32,2048]{2,1,0:T(8,128)} async-done(((f32[32,32,2048]{2,1,0:T(8,128)}), f32[32,32,2048]{2,1,0:T(8,128)}, u32[]{:S(2)}, u32[]{:S(2)}) %all-to-all-start) | async-done | bytes 8388640 | tf_op jit(solution)/shard_map/all_to_all | solution.py:59
  632.4 13.9 %fusion.6 = bf16[4,256,2048]{1,2,0:T(8,128)(2,1)} fusion(f32[7,256,2048]{1,2,0:T(8,128)} %get-tuple-element.6, f32[2048]{0:T(1024)S(1)} %bitcast.48, f32[2048]{0:T(1024)S(1)} %bitcast.50, f32[2048]{0:T(1024)S(1)} %bitcast.52, f32[2048]{0:T(1024)S(1)} %bitcast.46), kind=kLoop, calls=%fused_computation.17 | loop fusion | flops 16777216 | bytes 37781504 | tf_op jit(solution)/shard_map/convert_element_type | solution.py:54
  652.6 31.6 %fusion.29 = f32[2048,1024]{1,0:T(8,128)} fusion(f32[2048,2048]{1,0:T(8,128)} %reshape.91, bf16[1024,2048]{1,0:T(8,128)(2,1)} %bitcast.41), kind=kOutput, calls=%fused_computation.62 | convolution fusion | flops 51539607552 | bytes 29360128 | tf_op jit(solution)/shard_map/dot_general | solution.py:56
  694.1 123.1 %all-to-all-done.2 = f32[32,32,2048]{2,1,0:T(8,128)} async-done(((f32[32,32,2048]{2,1,0:T(8,128)}), f32[32,32,2048]{2,1,0:T(8,128)}, u32[]{:S(2)}, u32[]{:S(2)}) %all-to-all-start.2) | async-done | bytes 8388640 | tf_op jit(solution)/shard_map/all_to_all | solution.py:59
  821.0 10.8 stack_reshape.13
  831.8 15.4 %copy.48 = f32[1,2,16,32,2,4,256]{6,1,5,2,0,4,3:T(2,128)} copy(f32[1,2,16,32,2,4,256]{6,5,4,3,2,1,0:T(4,128)} %stack_reshape.13) | data formatting | bytes 16777216 | tf_op jit(solution)/shard_map/stack;reshape | solution.py:61
  847.2 10.8 stack_reshape.12
  858.0 15.4 %copy.47 = f32[1,2,16,32,2,4,256]{6,1,5,2,0,4,3:T(2,128)} copy(f32[1,2,16,32,2,4,256]{6,5,4,3,2,1,0:T(4,128)} %stack_reshape.12) | data formatting | bytes 16777216 | tf_op jit(solution)/shard_map/stack;reshape | solution.py:61
  873.4 10.8 stack_reshape.14
  884.2 15.4 %copy.49 = f32[1,2,16,32,2,4,256]{6,1,5,2,0,4,3:T(2,128)} copy(f32[1,2,16,32,2,4,256]{6,5,4,3,2,1,0:T(4,128)} %stack_reshape.14) | data formatting | bytes 16777216 | tf_op jit(solution)/shard_map/stack;reshape | solution.py:61
  899.6 106.1 %all-to-all-done.3 = f32[32,32,2048]{2,1,0:T(8,128)} async-done(((f32[32,32,2048]{2,1,0:T(8,128)}), f32[32,32,2048]{2,1,0:T(8,128)}, u32[]{:S(2)}, u32[]{:S(2)}) %all-to-all-start.3) | async-done | bytes 8388640 | tf_op jit(solution)/shard_map/all_to_all | solution.py:59
  1005.7 10.8 stack_reshape.15
  1016.5 14.5 %copy.50 = f32[1,2,16,32,2,4,256]{6,1,5,2,0,4,3:T(2,128)S(1)} copy(f32[1,2,16,32,2,4,256]{6,5,4,3,2,1,0:T(4,128)} %stack_reshape.15) | data formatting | bytes 16777216 | tf_op jit(solution)/shard_map/stack;reshape | solution.py:61
  1031.1 18.3 %maximum_bitcast_fusion = f32[32,2,4,16,4,2,256]{6,5,4,3,2,1,0:T(2,128)} fusion(f32[1,2,16,32,2,4,256]{6,1,5,2,0,4,3:T(2,128)S(1)} %copy.50, f32[1,2,16,32,2,4,256]{6,1,5,2,0,4,3:T(2,128)S(1)} %copy-done.1, f32[1,2,16,32,2,4,256]{6,1,5,2,0,4,3:T(2,128)} %copy.48, f32[1,2,16,32,2,4,256]{6,1,5,2,0,4,3:T(2,128)} %copy.47), kind=kLoop, calls=%fused_computation.1 | loop fusion | flops 25165824 | bytes 67108864 | tf_op jit(solution)/shard_map/transpose | solution.py:62
  1049.3 41.8 %reshape.96 = f32[32,2,256,512]{3,2,1,0:T(8,128)} reshape(f32[32,2,4,16,4,2,256]{6,5,4,3,2,1,0:T(2,128)} %maximum_bitcast_fusion) | data formatting | bytes 67108864 | tf_op jit(solution)/shard_map/reshape | solution.py:63
  1091.1 36.8 %fusion.1 = f32[32,512,512]{2,1,0:T(8,128)} fusion(f32[32,2,256,512]{3,2,1,0:T(8,128)} %reshape.96), kind=kOutput, calls=%fused_computation.5 | convolution fusion | flops 25769803776 | bytes 67108864 | tf_op jit(solution)/shard_map/cma,cmb->cab/dot_general | solution.py:65
  1127.9 62.6 %convolution_bitcast_fusion = f32[1,32,512,512]{3,2,1,0:T(8,128)} fusion(f32[32,2,256,512]{3,2,1,0:T(8,128)} %reshape.96), kind=kOutput, calls=%fused_computation.8 | convolution fusion | flops 51539607552 | bytes 67108864 | tf_op jit(solution)/shard_map/cpma,cpmb->cab/dot_general | solution.py:64
  1190.5 33.4 %copy.53 = f32[32,512,512]{1,2,0:T(8,128)} copy(f32[32,512,512]{2,1,0:T(8,128)} %fusion.1) | data formatting | bytes 67108864 | tf_op jit(solution)/shard_map/cma,cmb->cab/dot_general | solution.py:65
  1223.9 33.1 %fusion = f32[1,32,512,512]{3,2,1,0:T(8,128)} fusion(f32[32,512,512]{2,1,0:T(8,128)} %fusion.1, f32[32,512,512]{1,2,0:T(8,128)} %copy.53), kind=kLoop, calls=%fused_computation.3 | loop fusion | flops 8388608 | bytes 100663296 | tf_op jit(solution)/shard_map/stack | solution.py:67
  1257.0 44.9 %maximum_multiply_fusion = f32[2,32,512,512]{3,2,1,0:T(8,128)} fusion(f32[1,32,512,512]{3,2,1,0:T(8,128)} %fusion, f32[1,32,512,512]{3,2,1,0:T(8,128)} %convolution_bitcast_fusion), kind=kLoop, calls=%fused_computation | loop fusion | flops 33554432 | bytes 134217728 | tf_op jit(solution)/shard_map/div | solution.py:67
  (23 shorter events, 85.3 us)
Async XLA Ops:
  45.6 39.4 %copy-start = (bf16[256,32768]{0,1:T(8,128)(2,1)}, bf16[256,32768]{0,1:T(8,128)(2,1)S(1)}, u32[]{:S(2)}) copy-start(bf16[256,32768]{0,1:T(8,128)(2,1)S(1)} %convert_element_type.58) | copy-start | bytes 50331652
  47.6 85.9 %collective-permute-start = (bf16[3,256,2048]{1,2,0:T(8,128)(2,1)}, bf16[3,256,2048]{1,2,0:T(8,128)(2,1)S(1)}, u32[]{:S(2)}, u32[]{:S(2)}) collective-permute-start(bf16[3,256,2048]{1,2,0:T(8,128)(2,1)} %slice.121), channel_id=1, source_target_pairs={{0,1},{1,2},{2,3},{3,4},{4,5},{5,6},{6,7},{7,8},{8,9},{9,10},{10,1... | collective-permute-start | bytes 9437192 | tf_op jit(solution)/shard_map/ppermute | solution.py:15
  113.0 20.5 %copy-start.2 = (s32[4,2048]{1,0:T(4,128)S(1)}, s32[4,2048]{1,0:T(4,128)}, u32[]{:S(2)}) copy-start(s32[4,2048]{1,0:T(4,128)} %param.3) | copy-start | bytes 98308
  247.6 192.0 %all-to-all-start.1 = ((f32[32,32,2048]{2,1,0:T(8,128)}), f32[32,32,2048]{2,1,0:T(8,128)}, u32[]{:S(2)}, u32[]{:S(2)}) async-start(f32[32,32,2048]{2,1,0:T(8,128)} %reshape_reshape.13), calls=%async_computation.1 | async-start | bytes 16777216 | tf_op jit(solution)/shard_map/all_to_all | solution.py:59
  439.6 188.7 %all-to-all-start = ((f32[32,32,2048]{2,1,0:T(8,128)}), f32[32,32,2048]{2,1,0:T(8,128)}, u32[]{:S(2)}, u32[]{:S(2)}) async-start(f32[32,32,2048]{2,1,0:T(8,128)} %reshape_reshape.12), calls=%async_computation | async-start | bytes 16777216 | tf_op jit(solution)/shard_map/all_to_all | solution.py:59
  628.3 188.9 %all-to-all-start.2 = ((f32[32,32,2048]{2,1,0:T(8,128)}), f32[32,32,2048]{2,1,0:T(8,128)}, u32[]{:S(2)}, u32[]{:S(2)}) async-start(f32[32,32,2048]{2,1,0:T(8,128)} %reshape_reshape.14), calls=%async_computation.2 | async-start | bytes 16777216 | tf_op jit(solution)/shard_map/all_to_all | solution.py:59
  817.1 188.6 %all-to-all-start.3 = ((f32[32,32,2048]{2,1,0:T(8,128)}), f32[32,32,2048]{2,1,0:T(8,128)}, u32[]{:S(2)}, u32[]{:S(2)}) async-start(f32[32,32,2048]{2,1,0:T(8,128)} %reshape_reshape.15), calls=%async_computation.3 | async-start | bytes 16777216 | tf_op jit(solution)/shard_map/all_to_all | solution.py:59
  1016.5 14.5 %copy-start.1 = (f32[1,2,16,32,2,4,256]{6,1,5,2,0,4,3:T(2,128)S(1)}, f32[1,2,16,32,2,4,256]{6,1,5,2,0,4,3:T(2,128)}, u32[]{:S(2)}) copy-start(f32[1,2,16,32,2,4,256]{6,1,5,2,0,4,3:T(2,128)} %copy.49) | copy-start | bytes 25165828
where the time goes:
time: 1310 us; the launch traced here: 1300 us
  waiting for transfers between devices  503 us (38%)
  local copies, waits for them, and re-layouts  321 us (25%)
  other arithmetic  230 us (18%)
  matrix products  226 us (17%)
  starting transfers between devices  21.8 us (2%)
    all_to_all x4, waiting for transfers between devices, on_device(): lax.all_to_all(pieces, ('inp', 'tm'), split_axis=0, concat_axis=0, tiled=...  503 us
    dot_general x4, matrix products, on_device(): lax.dot_general(table, filtered, (((1,), (1,)), ((), ())), precision=high...  126 us
    another operation x8, local copies, waits for them, and re-layouts, on_device(): gathered = jnp.stack(collected, axis=0)  104 us
    dot_general x1, matrix products, on_device(): power = jnp.einsum('cpma,cpmb->cab', ordered, ordered, precision=highest)  62.6 us
    convert_element_type x2, other arithmetic, on_device(): filtered.astype(jnp.bfloat16)  52.6 us
    div x1, other arithmetic, on_device(): return jnp.stack([power, phase]) / total_spectra  44.9 us
    reshape x1, local copies, waits for them, and re-layouts, on_device(): ordered.reshape(chan_dev, 2, BLOCKS * tm_count * SPEC_BLK, all_inputs)  41.8 us
    another operation x4, local copies, waits for them, and re-layouts, on_device(): pieces = spectra.reshape(inp_count * tm_count, chan_dev, row_width)  39.7 us
  transfers between devices with their start and end apart: 5, of which 4 were waited for; matrix products, arithmetic and copies ran while one was open for 25% of the time, Pallas kernels for 0%

commit v1 on v0

v1 whole, which is shorter than its diff:
```python
import math

import jax
import jax.numpy as jnp
import numpy as np
from jax import lax
from jax.experimental import pallas as pl
from jax.experimental.pallas import tpu as pltpu
from jax.sharding import PartitionSpec as P

GROUPS = 8
F32 = jnp.float32
BF16 = jnp.bfloat16


def shifted(value, axis, steps):
    count = lax.axis_size(axis)
    initial, last = (max(0, -steps), min(count, count - steps))
    return lax.ppermute(value, axis, [(source, source + steps) for source in range(initial, last)])


def angle_tables(owners, chan_dev, frame_len):
    points = np.arange(frame_len)[None, :]
    coarse = (np.arange(owners)[:, None] * chan_dev * points) % frame_len
    fine = (np.arange(chan_dev)[:, None] * points) % frame_len
    turn = 2.0 * math.pi / frame_len
    return [
        np.stack([np.cos(part * turn), np.sin(part * turn)]).astype(np.float32) for part in (coarse, fine)
    ]


def build_table(coarse, fine, high, low, group, fine_count, owners):
    for j in range(fine_count):
        at = group * fine_count + j
        cos_f = fine[0, at : at + 1, :]
        sin_f = fine[1, at : at + 1, :]
        parts = (
            coarse[0] * cos_f - coarse[1] * sin_f,
            -(coarse[1] * cos_f + coarse[0] * sin_f),
        )
        for p, exact in enumerate(parts):
            rows = pl.ds((2 * j + p) * owners, owners)
            rounded = exact.astype(BF16)
            high[rows, :] = rounded
            low[rows, :] = (exact - rounded.astype(F32)).astype(BF16)


def transform(frame, high, low, spread, step, steps, fine_count, owners):
    contract = (((1,), (1,)), ((), ()))
    spectra = lax.dot_general(high[...], frame, contract, preferred_element_type=F32)
    spectra = spectra + lax.dot_general(low[...], frame, contract, preferred_element_type=F32)
    for part in range(2 * fine_count):
        piece = spectra[part * owners : (part + 1) * owners]
        for lane in range(spread.shape[0]):
            width = spread.shape[2]
            where = pl.ds(part * steps + step, owners, stride=2 * fine_count * steps)
            spread[lane, where, :] = piece[:, lane * width : (lane + 1) * width]


def flush(spread, out, owners):
    width = spread.shape[2]
    for lane in range(spread.shape[0]):
        out[:, :, lane * width : (lane + 1) * width] = (
            spread[lane].reshape(owners, -1, width).astype(BF16)
        )


def filter_kernel(samples, halo, taps, coarse, fine, filtered, out, high, low, spread, recent, *, group, fine_count, owners, steps, keep):
    step = pl.program_id(0)

    @pl.when(step == 0)
    def _():
        build_table(coarse, fine, high, low, group, fine_count, owners)
        for k in range(keep):
            recent[k] = halo[:, k * samples.shape[1] : (k + 1) * samples.shape[1]]

    weights = taps[...].astype(F32) * (1.0 / 16384.0)
    current = samples[...].astype(F32)
    total = weights[0:1] * recent[0].astype(F32)
    for k in range(1, keep):
        total = total + weights[k : k + 1] * recent[k].astype(F32)
    total = total + weights[keep : keep + 1] * current
    rounded = total.astype(BF16)
    filtered[0] = rounded
    for k in range(keep - 1):
        recent[k] = recent[k + 1]
    recent[keep - 1] = current.astype(BF16)
    transform(rounded, high, low, spread, step, steps, fine_count, owners)

    @pl.when(step == steps - 1)
    def _():
        flush(spread, out, owners)


def transform_kernel(filtered, coarse, fine, out, high, low, spread, *, group, fine_count, owners, steps):
    step = pl.program_id(0)

    @pl.when(step == 0)
    def _():
        build_table(coarse, fine, high, low, group, fine_count, owners)

    transform(filtered[0], high, low, spread, step, steps, fine_count, owners)

    @pl.when(step == steps - 1)
    def _():
        flush(spread, out, owners)


def correlate_kernel(*refs, inp_count, scale):
    arrived, out = refs[0], refs[-1]
    sources, rows, width = arrived.shape
    steps = rows // 2
    block = arrived[...]
    parts = []
    for p in range(2):
        part = block[:, p * steps : (p + 1) * steps, :]
        part = part.reshape(inp_count, (sources // inp_count) * steps, width)
        parts.append(jnp.concatenate([part[i] for i in range(inp_count)], axis=1))
    real, imag = parts
    real_t, imag_t = real.T, imag.T

    def product(left, right):
        return lax.dot_general(left, right, (((1,), (0,)), ((), ())), preferred_element_type=F32)

    out[0, 0] = (product(real_t, real) + product(imag_t, imag)) * scale
    out[1, 0] = (product(imag_t, real) - product(real_t, imag)) * scale


def on_device(samples, filter_taps):
    local_inputs = samples.shape[0]
    tap_count, frame_len = filter_taps.shape
    steps = samples.shape[1] // frame_len
    channels = frame_len // 2
    inp_count = lax.axis_size("inp")
    tm_count = lax.axis_size("tm")
    owners = inp_count * tm_count
    all_inputs = local_inputs * inp_count
    chan_dev = channels // owners
    groups = math.gcd(GROUPS, chan_dev)
    fine_count = chan_dev // groups
    total_spectra = steps * tm_count
    keep = tap_count - 1
    rows = 2 * fine_count * owners
    lane_width = min(128, local_inputs)
    lanes = local_inputs // lane_width
    coarse, fine = [jnp.asarray(t) for t in angle_tables(owners, chan_dev, frame_len)]

    tail = samples[:, (steps - keep) * frame_len :].astype(BF16)
    halo = shifted(tail, "tm", 1)

    scratch = [
        pltpu.VMEM((rows, frame_len), BF16),
        pltpu.VMEM((rows, frame_len), BF16),
        pltpu.VMEM((lanes, rows * steps, lane_width), F32),
    ]
    once = pl.Buffered(1)

    def whole(*shape):
        return pl.BlockSpec(shape, lambda s: (0,) * len(shape), pipeline_mode=once)

    piece = jax.ShapeDtypeStruct((owners, 2 * fine_count * steps, local_inputs), BF16)
    tables = [whole(*coarse.shape), whole(*fine.shape)]
    frame_spec = pl.BlockSpec((1, local_inputs, frame_len), lambda s: (s, 0, 0))
    filtered, first = pl.pallas_call(
        lambda *refs: filter_kernel(*refs, group=0, fine_count=fine_count, owners=owners, steps=steps, keep=keep),
        grid=(steps,),
        in_specs=[
            pl.BlockSpec((local_inputs, frame_len), lambda s: (0, s)),
            whole(local_inputs, keep * frame_len),
            whole(tap_count, frame_len),
            *tables,
        ],
        out_specs=[frame_spec, whole(*piece.shape)],
        out_shape=[jax.ShapeDtypeStruct((steps, local_inputs, frame_len), BF16), piece],
        scratch_shapes=scratch + [pltpu.VMEM((keep, local_inputs, frame_len), BF16)],
        name="filter_transform",
    )(samples, halo, filter_taps, coarse, fine)

    def exchange(value):
        return lax.all_to_all(value, ("inp", "tm"), split_axis=0, concat_axis=0, tiled=True)

    arrived = [exchange(first)]
    for group in range(1, groups):
        value = pl.pallas_call(
            lambda *refs, group=group: transform_kernel(
                *refs, group=group, fine_count=fine_count, owners=owners, steps=steps
            ),
            grid=(steps,),
            in_specs=[frame_spec, *tables],
            out_specs=whole(*piece.shape),
            out_shape=piece,
            scratch_shapes=scratch,
            name="transform",
        )(filtered, coarse, fine)
        arrived.append(exchange(value))

    result = None
    sources = owners
    for group in range(groups):
        value = arrived[group]
        block_inp = inp_count
        if local_inputs % 128:
            value = value.reshape(inp_count, tm_count, 2 * fine_count * steps, local_inputs)
            value = jnp.transpose(value, (1, 2, 0, 3)).reshape(tm_count, 2 * fine_count * steps, all_inputs)
            sources, block_inp = tm_count, 1
        operands = [value] if result is None else [value, result]
        specs = [pl.BlockSpec((sources, 2 * steps, value.shape[2]), lambda c: (0, c, 0))]
        if result is not None:
            specs.append(pl.BlockSpec(memory_space=pl.ANY))
        result = pl.pallas_call(
            lambda *refs, block_inp=block_inp: correlate_kernel(
                *refs, inp_count=block_inp, scale=1.0 / (frame_len * total_spectra)
            ),
            grid=(fine_count,),
            in_specs=specs,
            out_specs=pl.BlockSpec(
                (2, 1, all_inputs, all_inputs), lambda c, group=group: (0, group * fine_count + c, 0, 0)
            ),
            out_shape=jax.ShapeDtypeStruct((2, chan_dev, all_inputs, all_inputs), F32),
            input_output_aliases={} if result is None else {1: 0},
            name="correlate",
        )(*operands)
    return result


def solution(mesh):
    placed = (P("inp", "tm"), P())
    return jax.shard_map(
        on_device,
        mesh=mesh,
        in_specs=placed,
        out_specs=P(None, ("inp", "tm"), None, None),
        check_vma=False,
    )
```

time: 1310 us -> 523 us (0.40)
  local copies, waits for them, and re-layouts: 321 us -> 7.02 us
  waiting for transfers between devices: 503 us -> 211 us
  Pallas kernels: 0 us -> 235 us
  other arithmetic: 230 us -> 3.23 us
  matrix products: 226 us -> 0 us
  starting transfers between devices: 21.8 us -> 63.1 us
    all_to_all x4 -> x8, waiting for transfers between devices: 503 us -> 206 us  [exchange(): lax.all_to_all(value, ('inp', 'tm'), split_axis=0, concat_axis=0, tiled=T...]
    pallas_call x0 -> x16, Pallas kernels: none -> 235 us  [the longest x7 149 us: on_device(): pl.pallas_call(lambda *refs, group=group: transform_kernel(*refs, group=g...]
    dot_general x6 -> x0, matrix products: 226 us -> none  [the longest x4 126 us: on_device(): lax.dot_general(table, filtered, (((1,), (1,)), ((), ())), precision=high...]
    another operation x13 -> x0, local copies, waits for them, and re-layouts: 165 us -> none  [the longest x8 104 us: on_device(): gathered = jnp.stack(collected, axis=0)]
    convert_element_type x4 -> x0, other arithmetic: 92.1 us -> none  [the longest x2 52.6 us: on_device(): filtered.astype(jnp.bfloat16)]
    reshape x2 -> x0, local copies, waits for them, and re-layouts: 62.3 us -> none  [the longest x1 41.8 us: on_device(): ordered.reshape(chan_dev, 2, BLOCKS * tm_count * SPEC_BLK, all_inputs)]
    div x2 -> x0, other arithmetic: 44.9 us -> none  [the longest x1 44.9 us: on_device(): return jnp.stack([power, phase]) / total_spectra]
    all_to_all x4 -> x8, starting transfers between devices: 19.2 us -> 60.5 us  [exchange(): lax.all_to_all(value, ('inp', 'tm'), split_axis=0, concat_axis=0, tiled=T...]
  transfers between devices with their start and end apart: 5 -> 9, of which waited for: 4 -> 9; matrix products, arithmetic and copies ran while one was open for 25% -> 0% of each run, Pallas kernels for 0% -> 38%
where the time goes in v1:
time: 523 us; the launch traced here: 519 us
  Pallas kernels  235 us (45%)
  waiting for transfers between devices  211 us (40%)
  starting transfers between devices  63.1 us (12%)
  local copies, waits for them, and re-layouts  7.02 us (1%)
    all_to_all x8, waiting for transfers between devices, exchange(): lax.all_to_all(value, ('inp', 'tm'), split_axis=0, concat_axis=0, tiled=T...  206 us
    pallas_call x7, Pallas kernels, on_device(): pl.pallas_call(lambda *refs, group=group: transform_kernel(*refs, group=g...  149 us
    all_to_all x8, starting transfers between devices, exchange(): lax.all_to_all(value, ('inp', 'tm'), split_axis=0, concat_axis=0, tiled=T...  60.5 us
    pallas_call x8, Pallas kernels, on_device(): pl.pallas_call(lambda *refs, block_inp=block_inp: correlate_kernel(*refs,...  52.5 us
    pallas_call x1, Pallas kernels, on_device(): pl.pallas_call(lambda *refs: filter_kernel(*refs, group=0, fine_count=fin...  33.2 us
  transfers between devices with their start and end apart: 9, of which 9 were waited for; matrix products, arithmetic and copies ran while one was open for 0% of the time, Pallas kernels for 38%

profile of v1, /device:TPU:0, one launch (start us, length us, event | category | flops | bytes accessed | tf_op | source)
XLA Modules:
  0.0 518.9 jit_solution(8129055862011310265)
XLA Ops:
  0.0 3.2 slice_convert_fusion
  5.8 5.1 collective-permute-done.refs_1_
  12.6 33.2 %filter_transform.1 = (bf16[16,256,2048]{2,1,0:T(8,128)(2,1)}, bf16[32,128,256]{2,1,0:T(8,128)(2,1)}) custom-call(s32[256,32768]{1,0:T(8,128)} %refs_0_.1, bf16[256,6144]{1,0:T(8,128)(2,1)} %copy-done.4, s32[4,2048]{1,0:T(4,128)} %refs_2_.8, f32[2,32,2048]{2,1,0:T(8,128)} %constant.4.clone.refs_3_.refs_1_, f32[2,32,2048]{2,1,0:T(8,128)} %constant.5.clone.refs_4_.refs_2_), custom_call_target="tpu_custom_call" | custom-call | tf_op jit(solution)/shard_map/filter_transform/pallas_call | solution.py:164
  45.8 38.2 %all-to-all-start.7 = ((bf16[32,128,256]{2,1,0:T(8,128)(2,1)}), bf16[32,128,256]{2,1,0:T(8,128)(2,1)S(1)}, u32[]{:S(2)}, u32[]{:S(2)}) async-start(bf16[32,128,256]{2,1,0:T(8,128)(2,1)} %get-tuple-element.8), calls=%async_computation.7 | async-start | bytes 4194304 | tf_op jit(solution)/shard_map/all_to_all | solution.py:180
  84.0 21.3 %transform.13 = bf16[32,128,256]{2,1,0:T(8,128)(2,1)} custom-call(bf16[16,256,2048]{2,1,0:T(8,128)(2,1)} %get-tuple-element.7.refs_0_, f32[2,32,2048]{2,1,0:T(8,128)} %constant.4.clone.refs_3_.refs_1_, f32[2,32,2048]{2,1,0:T(8,128)} %constant.5.clone.refs_4_.refs_2_), custom_call_target="tpu_custom_call" | custom-call | tf_op jit(solution)/shard_map/transform/pallas_call | solution.py:184
  105.3 28.8 %all-to-all-done.7.refs_0_ = bf16[32,128,256]{2,1,0:T(8,128)(2,1)S(1)} async-done(((bf16[32,128,256]{2,1,0:T(8,128)(2,1)}), bf16[32,128,256]{2,1,0:T(8,128)(2,1)S(1)}, u32[]{:S(2)}, u32[]{:S(2)}) %all-to-all-start.7) | async-done | bytes 2097184 | tf_op jit(solution)/shard_map/all_to_all | solution.py:180
  138.1 21.3 %transform.12 = bf16[32,128,256]{2,1,0:T(8,128)(2,1)} custom-call(bf16[16,256,2048]{2,1,0:T(8,128)(2,1)} %get-tuple-element.7.refs_0_, f32[2,32,2048]{2,1,0:T(8,128)} %constant.4.clone.refs_3_.refs_1_, f32[2,32,2048]{2,1,0:T(8,128)} %constant.5.clone.refs_4_.refs_2_), custom_call_target="tpu_custom_call" | custom-call | tf_op jit(solution)/shard_map/transform/pallas_call | solution.py:184
  159.4 28.8 %all-to-all-done.6.refs_0_ = bf16[32,128,256]{2,1,0:T(8,128)(2,1)S(1)} async-done(((bf16[32,128,256]{2,1,0:T(8,128)(2,1)}), bf16[32,128,256]{2,1,0:T(8,128)(2,1)S(1)}, u32[]{:S(2)}, u32[]{:S(2)}) %all-to-all-start.6) | async-done | bytes 2097184 | tf_op jit(solution)/shard_map/all_to_all | solution.py:180
  189.6 3.5 all-to-all-start.5
  193.1 21.3 %transform.11 = bf16[32,128,256]{2,1,0:T(8,128)(2,1)} custom-call(bf16[16,256,2048]{2,1,0:T(8,128)(2,1)} %get-tuple-element.7.refs_0_, f32[2,32,2048]{2,1,0:T(8,128)} %constant.4.clone.refs_3_.refs_1_, f32[2,32,2048]{2,1,0:T(8,128)} %constant.5.clone.refs_4_.refs_2_), custom_call_target="tpu_custom_call" | custom-call | tf_op jit(solution)/shard_map/transform/pallas_call | solution.py:184
  214.4 28.8 %all-to-all-done.5.refs_0_ = bf16[32,128,256]{2,1,0:T(8,128)(2,1)} async-done(((bf16[32,128,256]{2,1,0:T(8,128)(2,1)}), bf16[32,128,256]{2,1,0:T(8,128)(2,1)}, u32[]{:S(2)}, u32[]{:S(2)}) %all-to-all-start.5) | async-done | bytes 2097184 | tf_op jit(solution)/shard_map/all_to_all | solution.py:180
  243.2 2.7 all-to-all-start.4
  245.9 21.3 %transform.10 = bf16[32,128,256]{2,1,0:T(8,128)(2,1)} custom-call(bf16[16,256,2048]{2,1,0:T(8,128)(2,1)} %get-tuple-element.7.refs_0_, f32[2,32,2048]{2,1,0:T(8,128)} %constant.4.clone.refs_3_.refs_1_, f32[2,32,2048]{2,1,0:T(8,128)} %constant.5.clone.refs_4_.refs_2_), custom_call_target="tpu_custom_call" | custom-call | tf_op jit(solution)/shard_map/transform/pallas_call | solution.py:184
  267.2 28.8 %all-to-all-done.4.refs_0_ = bf16[32,128,256]{2,1,0:T(8,128)(2,1)S(1)} async-done(((bf16[32,128,256]{2,1,0:T(8,128)(2,1)}), bf16[32,128,256]{2,1,0:T(8,128)(2,1)S(1)}, u32[]{:S(2)}, u32[]{:S(2)}) %all-to-all-start.4) | async-done | bytes 2097184 | tf_op jit(solution)/shard_map/all_to_all | solution.py:180
  297.4 3.7 all-to-all-start.3
  301.1 21.3 %transform.9 = bf16[32,128,256]{2,1,0:T(8,128)(2,1)} custom-call(bf16[16,256,2048]{2,1,0:T(8,128)(2,1)} %get-tuple-element.7.refs_0_, f32[2,32,2048]{2,1,0:T(8,128)} %constant.4.clone.refs_3_.refs_1_, f32[2,32,2048]{2,1,0:T(8,128)} %constant.5.clone.refs_4_.refs_2_), custom_call_target="tpu_custom_call" | custom-call | tf_op jit(solution)/shard_map/transform/pallas_call | solution.py:184
  322.4 28.6 %all-to-all-done.3.refs_0_ = bf16[32,128,256]{2,1,0:T(8,128)(2,1)} async-done(((bf16[32,128,256]{2,1,0:T(8,128)(2,1)}), bf16[32,128,256]{2,1,0:T(8,128)(2,1)}, u32[]{:S(2)}, u32[]{:S(2)}) %all-to-all-start.3) | async-done | bytes 2097184 | tf_op jit(solution)/shard_map/all_to_all | solution.py:180
  353.7 21.3 %transform.8 = bf16[32,128,256]{2,1,0:T(8,128)(2,1)} custom-call(bf16[16,256,2048]{2,1,0:T(8,128)(2,1)} %get-tuple-element.7.refs_0_, f32[2,32,2048]{2,1,0:T(8,128)} %constant.4.clone.refs_3_.refs_1_, f32[2,32,2048]{2,1,0:T(8,128)} %constant.5.clone.refs_4_.refs_2_), custom_call_target="tpu_custom_call" | custom-call | tf_op jit(solution)/shard_map/transform/pallas_call | solution.py:184
  375.0 28.9 %all-to-all-done.2.refs_0_ = bf16[32,128,256]{2,1,0:T(8,128)(2,1)S(1)} async-done(((bf16[32,128,256]{2,1,0:T(8,128)(2,1)}), bf16[32,128,256]{2,1,0:T(8,128)(2,1)S(1)}, u32[]{:S(2)}, u32[]{:S(2)}) %all-to-all-start.2) | async-done | bytes 2097184 | tf_op jit(solution)/shard_map/all_to_all | solution.py:180
  405.2 3.5 all-to-all-start.1
  408.7 21.3 %transform.7 = bf16[32,128,256]{2,1,0:T(8,128)(2,1)} custom-call(bf16[16,256,2048]{2,1,0:T(8,128)(2,1)} %get-tuple-element.7.refs_0_, f32[2,32,2048]{2,1,0:T(8,128)} %constant.4.clone.refs_3_.refs_1_, f32[2,32,2048]{2,1,0:T(8,128)} %constant.5.clone.refs_4_.refs_2_), custom_call_target="tpu_custom_call" | custom-call | tf_op jit(solution)/shard_map/transform/pallas_call | solution.py:184
  429.9 28.8 %all-to-all-done.1.refs_0_ = bf16[32,128,256]{2,1,0:T(8,128)(2,1)} async-done(((bf16[32,128,256]{2,1,0:T(8,128)(2,1)}), bf16[32,128,256]{2,1,0:T(8,128)(2,1)}, u32[]{:S(2)}, u32[]{:S(2)}) %all-to-all-start.1) | async-done | bytes 2097184 | tf_op jit(solution)/shard_map/all_to_all | solution.py:180
  458.8 3.5 all-to-all-start
  462.2 6.6 %correlate.8.refs_1_ = f32[2,32,512,512]{3,2,1,0:T(8,128)} custom-call(bf16[32,128,256]{2,1,0:T(8,128)(2,1)} %copy-done.3), custom_call_target="tpu_custom_call" | custom-call | tf_op jit(solution)/shard_map/correlate/pallas_call | solution.py:210
  468.8 6.6 %correlate.9.refs_1_ = f32[2,32,512,512]{3,2,1,0:T(8,128)} custom-call(bf16[32,128,256]{2,1,0:T(8,128)(2,1)} %copy-done, f32[2,32,512,512]{3,2,1,0:T(8,128)} %correlate.8.refs_1_), custom_call_target="tpu_custom_call", output_to_operand_aliasing={{}: (1, {})} | custom-call | tf_op jit(solution)/shard_map/correlate/pallas_call | solution.py:210
  475.4 6.6 %correlate.10.refs_1_ = f32[2,32,512,512]{3,2,1,0:T(8,128)} custom-call(bf16[32,128,256]{2,1,0:T(8,128)(2,1)} %all-to-all-done.5.refs_0_, f32[2,32,512,512]{3,2,1,0:T(8,128)} %correlate.9.refs_1_), custom_call_target="tpu_custom_call", output_to_operand_aliasing={{}: (1, {})} | custom-call | tf_op jit(solution)/shard_map/correlate/pallas_call | solution.py:210
  482.0 6.6 %correlate.11.refs_1_ = f32[2,32,512,512]{3,2,1,0:T(8,128)} custom-call(bf16[32,128,256]{2,1,0:T(8,128)(2,1)} %copy-done.1, f32[2,32,512,512]{3,2,1,0:T(8,128)} %correlate.10.refs_1_), custom_call_target="tpu_custom_call", output_to_operand_aliasing={{}: (1, {})} | custom-call | tf_op jit(solution)/shard_map/correlate/pallas_call | solution.py:210
  488.5 6.6 %correlate.12.refs_1_ = f32[2,32,512,512]{3,2,1,0:T(8,128)} custom-call(bf16[32,128,256]{2,1,0:T(8,128)(2,1)} %all-to-all-done.3.refs_0_, f32[2,32,512,512]{3,2,1,0:T(8,128)} %correlate.11.refs_1_), custom_call_target="tpu_custom_call", output_to_operand_aliasing={{}: (1, {})} | custom-call | tf_op jit(solution)/shard_map/correlate/pallas_call | solution.py:210
  495.1 6.6 %correlate.13.refs_1_ = f32[2,32,512,512]{3,2,1,0:T(8,128)} custom-call(bf16[32,128,256]{2,1,0:T(8,128)(2,1)} %copy-done.2, f32[2,32,512,512]{3,2,1,0:T(8,128)} %correlate.12.refs_1_), custom_call_target="tpu_custom_call", output_to_operand_aliasing={{}: (1, {})} | custom-call | tf_op jit(solution)/shard_map/correlate/pallas_call | solution.py:210
  501.6 6.6 %correlate.14.refs_1_ = f32[2,32,512,512]{3,2,1,0:T(8,128)} custom-call(bf16[32,128,256]{2,1,0:T(8,128)(2,1)} %all-to-all-done.1.refs_0_, f32[2,32,512,512]{3,2,1,0:T(8,128)} %correlate.13.refs_1_), custom_call_target="tpu_custom_call", output_to_operand_aliasing={{}: (1, {})} | custom-call | tf_op jit(solution)/shard_map/correlate/pallas_call | solution.py:210
  508.2 4.1 all-to-all-done.refs_0_
  512.3 6.6 %correlate.15 = f32[2,32,512,512]{3,2,1,0:T(8,128)} custom-call(bf16[32,128,256]{2,1,0:T(8,128)(2,1)} %all-to-all-done.refs_0_, f32[2,32,512,512]{3,2,1,0:T(8,128)} %correlate.14.refs_1_), custom_call_target="tpu_custom_call", output_to_operand_aliasing={{}: (1, {})} | custom-call | tf_op jit(solution)/shard_map/correlate/pallas_call | solution.py:210
  (13 shorter events, 15.1 us)
Async XLA Ops:
  3.2 7.7 %collective-permute-start = (bf16[256,6144]{1,0:T(8,128)(2,1)S(1)}, bf16[256,6144]{1,0:T(8,128)(2,1)S(1)}, u32[]{:S(2)}, u32[]{:S(2)}) collective-permute-start(bf16[256,6144]{1,0:T(8,128)(2,1)S(1)} %slice_convert_fusion), channel_id=1, source_target_pairs={{0,1},{1,2},{2,3},{3,4},{4,5},{5,6},{6,7},{7,8},{8,9},{9,10},{10,1... | collective-permute-start | bytes 9437192 | tf_op jit(solution)/shard_map/ppermute | solution.py:19
  10.9 1.6 copy-start.4
  45.8 88.3 %all-to-all-start.7 = ((bf16[32,128,256]{2,1,0:T(8,128)(2,1)}), bf16[32,128,256]{2,1,0:T(8,128)(2,1)S(1)}, u32[]{:S(2)}, u32[]{:S(2)}) async-start(bf16[32,128,256]{2,1,0:T(8,128)(2,1)} %get-tuple-element.8), calls=%async_computation.7 | async-start | bytes 4194304 | tf_op jit(solution)/shard_map/all_to_all | solution.py:180
  134.1 1.3 copy-start.3
  135.4 52.9 %all-to-all-start.6 = ((bf16[32,128,256]{2,1,0:T(8,128)(2,1)}), bf16[32,128,256]{2,1,0:T(8,128)(2,1)S(1)}, u32[]{:S(2)}, u32[]{:S(2)}) async-start(bf16[32,128,256]{2,1,0:T(8,128)(2,1)} %transform.13), calls=%async_computation.6 | async-start | bytes 4194304 | tf_op jit(solution)/shard_map/all_to_all | solution.py:180
  188.3 1.3 copy-start
  189.6 53.6 %all-to-all-start.5 = ((bf16[32,128,256]{2,1,0:T(8,128)(2,1)}), bf16[32,128,256]{2,1,0:T(8,128)(2,1)}, u32[]{:S(2)}, u32[]{:S(2)}) async-start(bf16[32,128,256]{2,1,0:T(8,128)(2,1)} %transform.12), calls=%async_computation.5 | async-start | bytes 4194304 | tf_op jit(solution)/shard_map/all_to_all | solution.py:180
  243.2 52.9 %all-to-all-start.4 = ((bf16[32,128,256]{2,1,0:T(8,128)(2,1)}), bf16[32,128,256]{2,1,0:T(8,128)(2,1)S(1)}, u32[]{:S(2)}, u32[]{:S(2)}) async-start(bf16[32,128,256]{2,1,0:T(8,128)(2,1)} %transform.11), calls=%async_computation.4 | async-start | bytes 4194304 | tf_op jit(solution)/shard_map/all_to_all | solution.py:180
  296.0 1.4 copy-start.1
  297.4 53.6 %all-to-all-start.3 = ((bf16[32,128,256]{2,1,0:T(8,128)(2,1)}), bf16[32,128,256]{2,1,0:T(8,128)(2,1)}, u32[]{:S(2)}, u32[]{:S(2)}) async-start(bf16[32,128,256]{2,1,0:T(8,128)(2,1)} %transform.10), calls=%async_computation.3 | async-start | bytes 4194304 | tf_op jit(solution)/shard_map/all_to_all | solution.py:180
  351.0 52.9 %all-to-all-start.2 = ((bf16[32,128,256]{2,1,0:T(8,128)(2,1)}), bf16[32,128,256]{2,1,0:T(8,128)(2,1)S(1)}, u32[]{:S(2)}, u32[]{:S(2)}) async-start(bf16[32,128,256]{2,1,0:T(8,128)(2,1)} %transform.9), calls=%async_computation.2 | async-start | bytes 4194304 | tf_op jit(solution)/shard_map/all_to_all | solution.py:180
  403.9 1.3 copy-start.2
  405.2 53.6 %all-to-all-start.1 = ((bf16[32,128,256]{2,1,0:T(8,128)(2,1)}), bf16[32,128,256]{2,1,0:T(8,128)(2,1)}, u32[]{:S(2)}, u32[]{:S(2)}) async-start(bf16[32,128,256]{2,1,0:T(8,128)(2,1)} %transform.8), calls=%async_computation.1 | async-start | bytes 4194304 | tf_op jit(solution)/shard_map/all_to_all | solution.py:180
  458.8 53.6 %all-to-all-start = ((bf16[32,128,256]{2,1,0:T(8,128)(2,1)}), bf16[32,128,256]{2,1,0:T(8,128)(2,1)}, u32[]{:S(2)}, u32[]{:S(2)}) async-start(bf16[32,128,256]{2,1,0:T(8,128)(2,1)} %transform.7), calls=%async_computation | async-start | bytes 4194304 | tf_op jit(solution)/shard_map/all_to_all | solution.py:180
